TPU v7x, 128 devices: a whole 4x4x4 slice. The times are simulated.
128 devices in a mesh: seq: 64 (over y, z, x), ch: 2 (over core).
Axes of the slice: x: 4, y: 4, z: 4, core: 2. Of those that a mesh axis runs over, the one named last changes fastest.
Arguments:
- cotangent: bfloat16 [16384, 2, 2048], P('seq', None, 'ch'), may hold values from -6 to 6
- conv_input: bfloat16 [16384, 2, 2048], P('seq', None, 'ch'), may hold values from -6 to 6
- decay_rate: bfloat16 [16384, 2048], P('seq', 'ch'), may hold values from 2.4414063e-06 to 0.7
- angle: float32 [2048], P('ch'), may hold values from -3.140625 to 3.140625
- conv_weight: float32 [4, 2, 2048], P(None, None, 'ch'), may hold values from -3 to 3
- in_weight: bfloat16 [4096, 2, 2048], P(None, None, 'ch'), may hold values from -0.09375 to 0.09375
Outputs:
- input_grad: bfloat16 [16384, 4096], P(('seq', 'ch'))
- channel_major: bfloat16 [2, 2048, 16384], P(None, ('ch', 'seq'))
- tap_grad: float32 [4, 2, 2048], P(None, None, 'ch')
All inputs are finite; a program needn't handle non-finite values.
Results may differ from a plain program's by a relative error of at most 0.0085.
Values may be sent and summed in bfloat16 or wider, within the bound.
A program may use at most 128 MiB of HBM per device.

v0:
```python
import jax
import jax.numpy as jnp
from jax import lax
from jax.sharding import PartitionSpec as P


def prefix(value, axis, join, neutral):
    count, mine = (lax.axis_size(axis), lax.axis_index(axis))
    pieces = jax.tree.map(lambda part: lax.all_gather(part, axis), value)
    pieces = jax.tree.map(lambda part: part[::-1], pieces)
    mine = count - 1 - mine
    total = jax.tree.map(
        lambda part, zero: jnp.full_like(part, 0) + jnp.asarray(zero, part.dtype), value, neutral
    )

    def hop(position, total):
        longer = join(total, jax.tree.map(lambda part: part[position], pieces))
        return jax.tree.map(lambda new, old: jnp.where(position < mine, new, old), longer, total)

    return lax.fori_loop(0, count - 1, hop, total)


def passed_along(array, axis, by):
    count = lax.axis_size(axis)
    pairs = [(i, i + by) for i in range(count) if 0 <= i + by < count]
    return lax.ppermute(array, axis, pairs)


def compose(earlier, later):
    outer_real, outer_imag, outer_shift_real, outer_shift_imag = earlier
    inner_real, inner_imag, inner_shift_real, inner_shift_imag = later
    return (
        inner_real * outer_real - inner_imag * outer_imag,
        inner_real * outer_imag + inner_imag * outer_real,
        inner_real * outer_shift_real - inner_imag * outer_shift_imag + inner_shift_real,
        inner_real * outer_shift_imag + inner_imag * outer_shift_real + inner_shift_imag,
    )


def local_block(cotangent, decay_rate, angle):
    rates = decay_rate.astype(jnp.float32)
    modulus = jnp.exp(-rates)
    mult_real = modulus * jnp.cos(angle)[None, :]
    mult_imag = -modulus * jnp.sin(angle)[None, :]
    step_real = jnp.concatenate([mult_real[1:], jnp.ones_like(mult_real[:1])], 0)
    step_imag = jnp.concatenate([mult_imag[1:], jnp.zeros_like(mult_imag[:1])], 0)
    upstream = cotangent.astype(jnp.float32)
    elements = (step_real[::-1], step_imag[::-1], upstream[::-1, 0], upstream[::-1, 1])
    scanned = lax.associative_scan(compose, elements, axis=0)
    prod_real, prod_imag, base_real, base_imag = [member[::-1] for member in scanned]
    return (rates, mult_real, mult_imag, prod_real, prod_imag, base_real, base_imag)


def on_device(cotangent, conv_input, decay_rate, angle, conv_weight, in_weight):
    rates, mult_real, mult_imag, prod_real, prod_imag, base_real, base_imag = local_block(
        cotangent, decay_rate, angle
    )
    length = cotangent.shape[0]
    width = cotangent.shape[2]
    map_real = mult_real[0] * prod_real[0] - mult_imag[0] * prod_imag[0]
    map_imag = mult_real[0] * prod_imag[0] + mult_imag[0] * prod_real[0]
    shift_real = mult_real[0] * base_real[0] - mult_imag[0] * base_imag[0]
    shift_imag = mult_real[0] * base_imag[0] + mult_imag[0] * base_real[0]
    ones_vec = jnp.ones((width,), jnp.float32)
    zero_vec = jnp.zeros((width,), jnp.float32)
    carried = prefix(
        (map_real, map_imag, shift_real, shift_imag),
        "seq",
        compose,
        (ones_vec, zero_vec, zero_vec, zero_vec),
    )
    carry_real = carried[2]
    carry_imag = carried[3]
    grad_real = base_real + prod_real * carry_real[None] - prod_imag * carry_imag[None]
    grad_imag = base_imag + prod_real * carry_imag[None] + prod_imag * carry_real[None]
    scaling = jnp.sqrt(-jnp.expm1(-2.0 * rates))
    conv_grad = jnp.stack([grad_real * scaling, grad_imag * scaling], 1)
    upper_rim = passed_along(conv_grad[:3], "seq", -1)
    extended = jnp.concatenate([conv_grad, upper_rim], 0)
    feature_sum = conv_weight[0][None] * extended[0:length]
    for tap_index in range(1, 4):
        feature_sum = (
            feature_sum + conv_weight[tap_index][None] * extended[tap_index : tap_index + length]
        )
    input_feat = feature_sum.astype(jnp.bfloat16)
    lower_rim = passed_along(conv_input[length - 3 :], "seq", 1)
    shifted_input = jnp.concatenate([lower_rim, conv_input], 0).astype(jnp.float32)
    taps = []
    for tap_index in range(4):
        taps.append(
            jnp.sum(conv_grad * shifted_input[3 - tap_index : 3 - tap_index + length], axis=0)
        )
    tap_grad = lax.psum(jnp.stack(taps, 0), "seq")
    layout = jnp.transpose(input_feat, (1, 2, 0))
    channel_major = lax.all_to_all(layout, "seq", split_axis=1, concat_axis=2, tiled=True)
    summed = lax.psum_scatter(
        lax.dot_general(
            input_feat, in_weight, (((1, 2), (1, 2)), ((), ())), preferred_element_type=jnp.float32
        ).astype(jnp.bfloat16),
        "ch",
        scatter_dimension=0,
        tiled=True,
    )
    return (summed, channel_major, tap_grad)


def solution(mesh):
    in_specs = (
        P("seq", None, "ch"),
        P("seq", None, "ch"),
        P("seq", "ch"),
        P("ch"),
        P(None, None, "ch"),
        P(None, None, "ch"),
    )
    out_specs = (P(("seq", "ch"), None), P(None, ("ch", "seq"), None), P(None, None, "ch"))
    return jax.shard_map(
        on_device, mesh=mesh, in_specs=in_specs, out_specs=out_specs, check_vma=False
    )
```

profile of v0, /device:TPU:0, one launch (start us, length us, event | category | flops | bytes accessed | tf_op | source)
XLA Modules:
  0.0 1332.5 jit_solution(1409491636093875351)
XLA Ops:
  7.2 1.3 slice.741
  8.5 4.1 collective-permute-start.1
  13.3 1.3 fusion.18
  14.7 1.0 copy-done.4
  15.9 1.5 slice.586
  17.3 1.5 slice.575
  18.8 1.5 slice.573
  20.4 1.5 slice.691
  21.9 1.4 slice.588
  23.3 1.5 slice.580
  26.5 1.5 slice.732
  29.1 1.5 slice.696
  30.6 1.5 slice.584
  32.1 1.4 slice.578
  33.6 2.7 slice.587
  36.2 2.7 slice.576
  38.9 2.6 slice.581
  41.5 2.7 slice.589
  44.2 2.3 add_add_fusion.1
  51.6 1.2 add_add_fusion.3
  64.2 1.0 pad.251
  65.2 1.4 pad.253
  68.3 1.7 add.569
  70.7 0.9 multiply_add_fusion.2
  72.6 1.7 pad.254
  74.3 1.7 pad.256
  76.0 1.7 pad.255
  77.6 1.7 pad.257
  81.3 0.9 add.572
  83.1 1.3 multiply_subtract_fusion
  84.4 1.2 add_add_fusion
  86.9 2.1 pad.229
  89.0 4.6 pad.263
  93.6 2.3 add.579
  96.8 1.1 add.551
  99.1 2.1 pad.261
  101.2 1.9 concatenate.124
  103.1 4.6 pad.260
  107.7 2.3 add.575
  110.8 1.1 add.573
  111.9 8.9 rev.34
  120.9 5.2 rev.41
  126.1 176.5 %all-gather.3 = f32[64,1,1024]{2,1,0:T(1,128)S(1)} all-gather(f32[1,1,1024]{2,1,0:T(1,128)S(1)} %get-tuple-element.198), channel_id=1, replica_groups=mesh['seq'=64,'ch'=2] {'seq'}, dimensions={0}, use_global_device_ids=true | all-gather | bytes 266240 | tf_op jit(solution)/shard_map/all_gather | solution.py:9
  302.7 2.6 rev.39
  305.3 170.6 %all-gather.2 = f32[64,1,1024]{2,1,0:T(1,128)S(1)} all-gather(f32[1,1,1024]{2,1,0:T(1,128)S(1)} %get-tuple-element.199), channel_id=1, replica_groups=mesh['seq'=64,'ch'=2] {'seq'}, dimensions={0}, use_global_device_ids=true | all-gather | bytes 266240 | tf_op jit(solution)/shard_map/all_gather | solution.py:9
  476.0 2.5 rev.38
  479.1 5.2 rev.40
  484.3 172.6 %all-gather.1 = f32[64,1,1024]{2,1,0:T(1,128)S(1)} all-gather(f32[1,1,1024]{2,1,0:T(1,128)S(1)} %get-tuple-element.200), channel_id=1, replica_groups=mesh['seq'=64,'ch'=2] {'seq'}, dimensions={0}, use_global_device_ids=true | all-gather | bytes 266240 | tf_op jit(solution)/shard_map/all_gather | solution.py:9
  656.9 2.5 rev.37
  659.5 170.6 %all-gather = f32[64,1,1024]{2,1,0:T(1,128)S(1)} all-gather(f32[1,1,1024]{2,1,0:T(1,128)S(1)} %get-tuple-element.201), channel_id=1, replica_groups=mesh['seq'=64,'ch'=2] {'seq'}, dimensions={0}, use_global_device_ids=true | all-gather | bytes 266240 | tf_op jit(solution)/shard_map/all_gather | solution.py:9
  830.1 2.5 rev.36
  832.7 102.7 %while.16 = (s32[]{:T(128)}, f32[1024]{0:T(1024)S(1)}, f32[1024]{0:T(1024)S(1)}, s32[]{:T(128)}, f32[64,1024]{1,0:T(8,128)}, /*index=5*/f32[64,1024]{1,0:T(8,128...) while((s32[]{:T(128)}, f32[1024]{0:T(1024)S(1)}, f32[1024]{0:T(1024)S(1)}, ...), condition=%wide.region_1.2_spmd.clone, body=%wide.region_0.1_spmd.clone.sunk | while | flops 12292 | bytes 65673 | solution.py:20
  935.4 2.4 fusion.23
  938.5 1.1 copy.28
  939.6 1.3 collective-permute-start
  941.0 1.8 maximum_convert_fusion
  942.8 2.6 collective-permute-done
  945.3 1.9 pad_maximum_fusion.1
  947.3 8.0 fusion.11
  955.2 12.7 fusion.5
  967.9 3.1 copy.31
  971.0 4.7 all-to-all-start
  975.7 348.7 %psum.7 = f32[4,2,1024]{2,1,0:T(2,128)} all-reduce(f32[4,2,1024]{2,1,0:T(2,128)S(1)} %pad_maximum_fusion.20), channel_id=1, replica_groups=mesh['seq'=64,'ch'=2] {'seq'}, use_global_device_ids=true, to_apply=%region_7.8 | all-reduce | flops 8192 | bytes 65536 | tf_op jit(solution)/shard_map/psum | solution.py:93
  1324.6 1.0 copy.38
  (510 shorter events, 131.8 us)
Async XLA Ops:
  7.2 1318.5 %reduce-scatter.2.cloned.1.call-start = ((), (), s32[]{:S(2)}) async-start(), calls=%async_computation.2 | async-start | bytes 3145728 | tf_op jit(solution)/shard_map/reduce_scatter | solution.py:96
  8.5 932.4 %collective-permute-start.1 = (bf16[3,2,1024]{2,1,0:T(2,128)(2,1)}, bf16[3,2,1024]{2,1,0:T(2,128)(2,1)}, u32[]{:S(2)}, u32[]{:S(2)}) collective-permute-start(bf16[3,2,1024]{2,1,0:T(2,128)(2,1)} %slice.741), channel_id=1, source_target_pairs={{0,2},{2,4},{4,6},{6,8},{8,10},{10,12},{12,14},{14,16},{16,18},{18... | collective-permute-start | bytes 36872 | tf_op jit(solution)/shard_map/ppermute | solution.py:26
  14.7 1.0 copy-start.4
  14.7 5.5 copy-start.5
  20.4 4.4 copy-start.24
  29.1 4.4 copy-start.19
  29.1 7.1 copy-start.18
  33.5 5.3 copy-start.21
  33.6 8.0 copy-start.20
  56.1 1.5 copy-start.16
  56.4 1.6 copy-start.17
  59.8 2.8 copy-start.40
  61.9 3.3 copy-start.34
  61.9 4.8 copy-start.33
  62.7 4.0 copy-start.35
  62.7 4.0 copy-start.39
  66.8 3.9 copy-start.11
  67.6 4.0 copy-start.25
  67.6 4.0 copy-start.26
  70.7 1.1 copy-start.38
  71.6 1.0 copy-start.32
  71.6 1.0 copy-start.37
  71.6 2.6 copy-start.31
  71.8 4.2 copy-start.30
  71.9 5.8 copy-start.29
  74.2 5.2 copy-start.28
  74.3 5.2 copy-start.27
  79.6 1.8 copy-start.1
  79.6 1.8 copy-start.3
  79.6 2.6 copy-start
  79.6 2.6 copy-start.2
  83.1 1.3 copy-start.12
  83.1 1.3 copy-start.13
  84.4 1.2 copy-start.42
  85.7 1.0 copy-start.15
  85.7 1.0 copy-start.41
  95.9 2.0 copy-start.22
  97.9 1.0 copy-start.14
  110.8 10.1 copy-start.6
  120.9 357.6 %copy-start.8 = (f32[256,1024]{1,0:T(8,128)S(1)}, f32[256,1024]{1,0:T(8,128)}, u32[]{:S(2)}) copy-start(f32[256,1024]{1,0:T(8,128)} %add.573) | copy-start | bytes 3145732
  302.7 176.3 %copy-start.7 = (f32[256,1024]{1,0:T(8,128)S(1)}, f32[256,1024]{1,0:T(8,128)}, u32[]{:S(2)}) copy-start(f32[256,1024]{1,0:T(8,128)} %add.575) | copy-start | bytes 3145732
  484.2 451.1 %copy-start.9 = (f32[256,1024]{1,0:T(8,128)S(1)}, f32[256,1024]{1,0:T(8,128)}, u32[]{:S(2)}) copy-start(f32[256,1024]{1,0:T(8,128)} %rev.34) | copy-start | bytes 3145732
  484.3 451.1 %copy-start.10 = (f32[256,1024]{1,0:T(8,128)S(1)}, f32[256,1024]{1,0:T(8,128)}, u32[]{:S(2)}) copy-start(f32[256,1024]{1,0:T(8,128)} %rev.41) | copy-start | bytes 3145732
  938.5 2.4 copy-start.36
  938.5 2.5 copy-start.23
  939.6 5.7 collective-permute-start
  971.0 353.4 %all-to-all-start = ((bf16[2,1024,256]{2,0,1:T(2,128)(2,1)}), bf16[2,1024,256]{2,0,1:T(2,128)(2,1)S(1)}, u32[]{:S(2)}, u32[]{:S(2)}) async-start(bf16[2,1024,256]{2,0,1:T(2,128)(2,1)} %copy.31), calls=%async_computation.1 | async-start | bytes 2097152 | tf_op jit(solution)/shard_map/all_to_all | solution.py:95
Sparse Core Ops, SparseCore 0:
  968.0 7.8 reduce-scatter.1
where the time goes:
time: 1340 us; the launch traced here: 1330 us
  blocking collectives  1040 us (78%)
  local copies, waits for them, and re-layouts  205 us (15%)
  other arithmetic  44.8 us (3%)
  between operations  15.7 us (1%)
    all_gather x4, blocking collectives, prefix(): pieces = jax.tree.map(lambda part: lax.all_gather(part, axis), value)  690 us
    psum x1, blocking collectives, on_device(): tap_grad = lax.psum(jnp.stack(taps, 0), 'seq')  349 us
    dynamic_slice x126, local copies, waits for them, and re-layouts, hop(): longer = join(total, jax.tree.map(lambda part: part[position], pieces))  99.6 us
    slice x110, local copies, waits for them, and re-layouts, local_block(): scanned = lax.associative_scan(compose, elements, axis=0)  36.3 us
  transfers between devices with their start and end apart: 4, of which 1 were waited for; matrix products, arithmetic and copies ran while one was open for 18% of the time, Pallas kernels for 0%

commit v1 on v0

--- a/solution.py
+++ b/solution.py
@@ -2,6 +2,12 @@
 import jax.numpy as jnp
 from jax import lax
 from jax.sharding import PartitionSpec as P
+
+
+def gather_and_add(block, axis):
+    parts = lax.all_gather(block, axis, axis=0, tiled=False)
+    total = parts.sum(axis=0)
+    return total
 
 
 def prefix(value, axis, join, neutral):
@@ -90,7 +96,7 @@
         taps.append(
             jnp.sum(conv_grad * shifted_input[3 - tap_index : 3 - tap_index + length], axis=0)
         )
-    tap_grad = lax.psum(jnp.stack(taps, 0), "seq")
+    tap_grad = gather_and_add(jnp.stack(taps, 0), "seq")
     layout = jnp.transpose(input_feat, (1, 2, 0))
     channel_major = lax.all_to_all(layout, "seq", split_axis=1, concat_axis=2, tiled=True)
     summed = lax.psum_scatter(

time: 1340 us -> 1040 us (0.78)
  blocking collectives: 1040 us -> 710 us
  waiting for transfers between devices: 2.59 us -> 28.1 us
    psum x1 -> x0, blocking collectives: 349 us -> none  [on_device(): tap_grad = lax.psum(jnp.stack(taps, 0), 'seq')]
    all_gather x0 -> x1, waiting for transfers between devices: none -> 25.5 us  [gather_and_add(): parts = lax.all_gather(block, axis, axis=0, tiled=False)]
    all_to_all x0 -> x1, blocking collectives: none -> 19.3 us  [on_device(): lax.all_to_all(layout, 'seq', split_axis=1, concat_axis=2, tiled=True)]
  transfers between devices with their start and end apart: 4 -> 4, of which waited for: 1 -> 2; matrix products, arithmetic and copies ran while one was open for 18% -> 24% of each run, Pallas kernels for 0% -> 0%
where the time goes in v1:
time: 1040 us; the launch traced here: 1030 us
  blocking collectives  710 us (68%)
  local copies, waits for them, and re-layouts  205 us (20%)
  other arithmetic  48.4 us (5%)
  waiting for transfers between devices  28.1 us (3%)
  between operations  17.1 us (2%)
  matrix products  12.7 us (1%)
    all_gather x4, blocking collectives, prefix(): pieces = jax.tree.map(lambda part: lax.all_gather(part, axis), value)  690 us
    dynamic_slice x126, local copies, waits for them, and re-layouts, hop(): longer = join(total, jax.tree.map(lambda part: part[position], pieces))  99.6 us
    slice x110, local copies, waits for them, and re-layouts, local_block(): scanned = lax.associative_scan(compose, elements, axis=0)  36.4 us
    all_gather x1, waiting for transfers between devices, gather_and_add(): parts = lax.all_gather(block, axis, axis=0, tiled=False)  25.5 us
    pad x56, local copies, waits for them, and re-layouts, local_block(): scanned = lax.associative_scan(compose, elements, axis=0)  24.1 us
  transfers between devices with their start and end apart: 4, of which 2 were waited for; matrix products, arithmetic and copies ran while one was open for 24% of the time, Pallas kernels for 0%

profile of v1, /device:TPU:0, one launch (start us, length us, event | category | flops | bytes accessed | tf_op | source)
XLA Modules:
  0.0 1028.8 jit_solution(15409342507324348460)
XLA Ops:
  8.0 1.3 slice.741
  9.4 4.1 collective-permute-start.1
  14.2 1.3 fusion.18
  15.5 1.0 copy-done.4
  16.7 1.5 slice.586
  18.2 1.5 slice.575
  19.7 1.5 slice.573
  21.3 1.5 slice.691
  22.8 1.5 slice.588
  24.2 1.5 slice.580
  27.4 1.6 slice.732
  30.1 1.5 slice.696
  31.6 1.5 slice.584
  33.1 1.5 slice.578
  34.5 2.6 slice.587
  37.2 2.7 slice.576
  39.8 2.7 slice.581
  42.5 2.7 slice.589
  45.2 2.3 add_add_fusion.1
  52.6 1.2 add_add_fusion.3
  65.2 1.0 pad.251
  66.1 1.4 pad.253
  69.2 1.7 add.567
  71.6 0.9 multiply_add_fusion.2
  73.5 1.7 pad.254
  75.2 1.7 pad.256
  77.0 1.7 pad.255
  78.6 1.6 pad.257
  84.1 1.3 multiply_subtract_fusion
  85.4 1.2 add_add_fusion
  87.9 2.1 pad.229
  90.0 4.6 pad.263
  94.6 2.3 add.577
  97.8 1.1 add.549
  100.1 2.1 pad.261
  102.2 1.9 concatenate.124
  104.1 4.6 pad.260
  108.7 2.3 add.573
  111.8 1.1 add.571
  112.9 8.9 rev.34
  121.8 5.2 rev.41
  127.1 176.6 %all-gather.4 = f32[64,1,1024]{2,1,0:T(1,128)S(1)} all-gather(f32[1,1,1024]{2,1,0:T(1,128)S(1)} %get-tuple-element.198), channel_id=1, replica_groups=mesh['seq'=64,'ch'=2] {'seq'}, dimensions={0}, use_global_device_ids=true | all-gather | bytes 266240 | tf_op jit(solution)/shard_map/all_gather | solution.py:15
  303.7 2.6 rev.39
  306.3 170.6 %all-gather.3 = f32[64,1,1024]{2,1,0:T(1,128)S(1)} all-gather(f32[1,1,1024]{2,1,0:T(1,128)S(1)} %get-tuple-element.199), channel_id=1, replica_groups=mesh['seq'=64,'ch'=2] {'seq'}, dimensions={0}, use_global_device_ids=true | all-gather | bytes 266240 | tf_op jit(solution)/shard_map/all_gather | solution.py:15
  477.0 2.6 rev.38
  480.1 5.2 rev.40
  485.3 172.6 %all-gather.2 = f32[64,1,1024]{2,1,0:T(1,128)S(1)} all-gather(f32[1,1,1024]{2,1,0:T(1,128)S(1)} %get-tuple-element.200), channel_id=1, replica_groups=mesh['seq'=64,'ch'=2] {'seq'}, dimensions={0}, use_global_device_ids=true | all-gather | bytes 266240 | tf_op jit(solution)/shard_map/all_gather | solution.py:15
  657.9 2.5 rev.37
  660.5 170.6 %all-gather.1 = f32[64,1,1024]{2,1,0:T(1,128)S(1)} all-gather(f32[1,1,1024]{2,1,0:T(1,128)S(1)} %get-tuple-element.201), channel_id=1, replica_groups=mesh['seq'=64,'ch'=2] {'seq'}, dimensions={0}, use_global_device_ids=true | all-gather | bytes 266240 | tf_op jit(solution)/shard_map/all_gather | solution.py:15
  831.1 2.5 rev.36
  833.7 102.7 %while.16 = (s32[]{:T(128)}, f32[1024]{0:T(1024)S(1)}, f32[1024]{0:T(1024)S(1)}, s32[]{:T(128)}, f32[64,1024]{1,0:T(8,128)}, /*index=5*/f32[64,1024]{1,0:T(8,128...) while((s32[]{:T(128)}, f32[1024]{0:T(1024)S(1)}, f32[1024]{0:T(1024)S(1)}, ...), condition=%wide.region_1.2_spmd.clone, body=%wide.region_0.1_spmd.clone.sunk | while | flops 12292 | bytes 65673 | solution.py:26
  936.4 2.4 fusion.23
  939.5 1.1 copy.28
  940.6 1.3 collective-permute-start
  942.0 1.8 maximum_convert_fusion
  943.8 2.6 collective-permute-done
  946.3 1.9 pad_maximum_fusion.1
  948.3 8.0 fusion.11
  957.2 12.7 %fusion.5 = bf16[256,4096]{1,0:T(8,128)(2,1)} fusion(bf16[4096,2,1024]{2,1,0:T(2,128)(2,1)} %param.13, bf16[256,2,1024]{2,1,0:T(2,128)(2,1)S(1)} %get-tuple-element.208), kind=kOutput, calls=%fused_computation.9 | convolution fusion | flops 4296015872 | bytes 19922944 | tf_op jit(solution)/shard_map/dot_general | solution.py:103
  969.9 2.6 copy.31
  972.6 19.3 %all_to_all.18 = bf16[2,1024,256]{2,0,1:T(2,128)(2,1)S(1)} all-to-all(bf16[2,1024,256]{2,0,1:T(2,128)(2,1)S(1)} %copy.31), channel_id=1, replica_groups=mesh['seq'=64,'ch'=2] {'seq'}, dimensions={1} | all-to-all | bytes 2097152 | tf_op jit(solution)/shard_map/all_to_all | solution.py:101
  992.0 1.0 copy.38
  993.0 25.5 %all-gather.7.cloned.1.call-done = f32[256,2,1024]{2,1,0:T(2,128)} async-done(((f32[4,2,1024]{2,1,0:T(2,128)}), f32[256,2,1024]{2,1,0:T(2,128)}) %all-gather.7.cloned.1.call-update) | async-done | bytes 2097168 | tf_op jit(solution)/shard_map/all_gather | solution.py:8
  1018.5 2.9 reduce_sum.49
  (512 shorter events, 133.6 us)
Async XLA Ops:
  8.0 1010.5 %all-gather.7.cloned.1.call-start = ((), (), s32[]{:S(2)}) async-start(), calls=%async_computation.3 | async-start | bytes 2129920 | tf_op jit(solution)/shard_map/all_gather | solution.py:8
  9.4 932.6 %collective-permute-start.1 = (bf16[3,2,1024]{2,1,0:T(2,128)(2,1)}, bf16[3,2,1024]{2,1,0:T(2,128)(2,1)}, u32[]{:S(2)}, u32[]{:S(2)}) collective-permute-start(bf16[3,2,1024]{2,1,0:T(2,128)(2,1)} %slice.741), channel_id=1, source_target_pairs={{0,2},{2,4},{4,6},{6,8},{8,10},{10,12},{12,14},{14,16},{16,18},{18... | collective-permute-start | bytes 36872 | tf_op jit(solution)/shard_map/ppermute | solution.py:32
  15.5 1.0 copy-start.4
  15.5 5.6 copy-start.5
  21.3 4.4 copy-start.24
  30.0 4.5 copy-start.19
  30.1 7.1 copy-start.18
  34.5 5.3 copy-start.21
  34.5 8.0 copy-start.20
  57.1 1.5 copy-start.16
  57.4 1.6 copy-start.17
  60.8 2.8 copy-start.40
  62.9 3.3 copy-start.34
  62.9 4.8 copy-start.33
  63.6 4.0 copy-start.35
  63.6 4.0 copy-start.39
  67.7 3.9 copy-start.11
  68.5 4.0 copy-start.25
  68.5 4.0 copy-start.26
  71.6 1.1 copy-start.38
  72.6 1.0 copy-start.32
  72.6 1.0 copy-start.37
  72.6 2.6 copy-start.31
  72.8 4.2 copy-start.30
  72.8 5.8 copy-start.29
  75.2 5.2 copy-start.28
  75.2 5.2 copy-start.27
  80.5 1.8 copy-start.1
  80.6 1.8 copy-start.3
  80.6 2.6 copy-start
  80.6 2.6 copy-start.2
  84.1 1.3 copy-start.12
  84.1 1.3 copy-start.13
  85.4 1.2 copy-start.42
  86.6 1.0 copy-start.15
  86.6 1.0 copy-start.41
  96.9 2.0 copy-start.22
  98.9 1.0 copy-start.14
  111.8 10.0 copy-start.6
  121.8 357.7 %copy-start.8 = (f32[256,1024]{1,0:T(8,128)S(1)}, f32[256,1024]{1,0:T(8,128)}, u32[]{:S(2)}) copy-start(f32[256,1024]{1,0:T(8,128)} %add.571) | copy-start | bytes 3145732
  303.7 176.4 %copy-start.7 = (f32[256,1024]{1,0:T(8,128)S(1)}, f32[256,1024]{1,0:T(8,128)}, u32[]{:S(2)}) copy-start(f32[256,1024]{1,0:T(8,128)} %add.573) | copy-start | bytes 3145732
  485.3 451.1 %copy-start.9 = (f32[256,1024]{1,0:T(8,128)S(1)}, f32[256,1024]{1,0:T(8,128)}, u32[]{:S(2)}) copy-start(f32[256,1024]{1,0:T(8,128)} %rev.34) | copy-start | bytes 3145732
  485.3 451.1 %copy-start.10 = (f32[256,1024]{1,0:T(8,128)S(1)}, f32[256,1024]{1,0:T(8,128)}, u32[]{:S(2)}) copy-start(f32[256,1024]{1,0:T(8,128)} %rev.41) | copy-start | bytes 3145732
  939.5 2.4 copy-start.36
  939.5 2.5 copy-start.23
  940.6 5.7 collective-permute-start
  956.9 64.4 %reduce-scatter.2.cloned.1.call-start = ((), (), s32[]{:S(2)}) async-start(), calls=%async_computation.2 | async-start | bytes 3145728 | tf_op jit(solution)/shard_map/reduce_scatter | solution.py:102
Sparse Core Ops, SparseCore 0:
  957.1 61.3 all-gather.6
Sparse Core Ops, SparseCore 1:
  970.0 7.7 reduce-scatter.1
